TPU v7x, 512 devices: a whole 4x4x16 slice. The times are simulated.
512 devices in a mesh: dp: 32 (over z, core), seq: 16 (over y, x).
Axes of the slice: x: 4, y: 4, z: 16, core: 2. Of those that a mesh axis runs over, the one named last changes fastest.
Arguments:
- features: bfloat16 [32, 3072, 1024], P('dp', 'seq'), may hold values from -18 to 18
- qkv_weight: bfloat16 [1024, 3072], P('dp'), may hold values from -1 to 1
- cotangent: bfloat16 [32, 3072, 1024], P('dp', 'seq'), may hold values from -6 to 6
- node_order: int32 [32, 3072], P('dp'), may hold values from 0 to 3071, as said below
- blocks: int32 [32, 48, 8], P('dp'), may hold values from 0 to 47, as said below
- counts: int32 [32, 48], P('dp'), may hold values from 1 to 8, as said below
Outputs:
- attended: bfloat16 [32, 3072, 1024], P('dp', 'seq')
- grad_features: bfloat16 [32, 3072, 1024], P('dp', 'seq')
- grad_weight: float32 [1024, 3072], P('dp', 'seq')
Inputs may be any that keep to these rules, and one draw needn't show every extreme that they name: Every row of node_order lists each node of the subgraph once. blocks[g, c, 0] is c, and the 8 entries of a row are distinct clusters; slots at or beyond counts[g, c] are unused. `counts`: every subgraph has a cluster with all 8 slots live.
All inputs are finite; a program needn't handle non-finite values.
Results may differ from a plain program's by a relative error of at most 0.03.
Values may be sent and summed in bfloat16 or wider, within the bound.
No kernel may reach another device: no remote copies, remote signals or barrier semaphores. Data moves between devices by JAX's collectives and lax.ppermute only.
A program may use at most 128 MiB of HBM per device.

v0:
```python
import math
import jax
import jax.numpy as jnp
from jax import lax
from jax.sharding import PartitionSpec as P

HEADS = 16
HD = 64


def attend(query, key_in, value, grad_out, blocks, counts):
    cluster_count, slot_count = blocks.shape
    node_count, head_width = query.shape
    block_rows = node_count // cluster_count
    in_group = math.gcd(cluster_count, 8)
    runs_total = cluster_count // in_group
    score_scale = 1.0 / math.sqrt(head_width)
    key_blocks = key_in.reshape(cluster_count, block_rows, head_width)
    value_blocks = value.reshape(cluster_count, block_rows, head_width)
    inputs_all = (
        query.reshape(runs_total, in_group, block_rows, head_width),
        grad_out.reshape(runs_total, in_group, block_rows, head_width),
        blocks.reshape(runs_total, in_group, slot_count),
        counts.reshape(runs_total, in_group),
    )

    def group_step(totals, inputs_now):
        grad_key, grad_value = totals
        query_block, grad_block, block_ids, live_count = inputs_now
        key_rows = key_blocks[block_ids].reshape(in_group, slot_count * block_rows, head_width)
        value_rows = value_blocks[block_ids].reshape(in_group, slot_count * block_rows, head_width)
        is_live = jnp.repeat(
            jnp.arange(slot_count)[None, :] < live_count[:, None], block_rows, axis=1
        )[:, None, :]
        scores = (
            jnp.einsum("cqe,cke->cqk", query_block, key_rows, preferred_element_type=jnp.float32)
            * score_scale
        )
        scores = jnp.where(is_live, scores, -1e30)
        row_max = jnp.max(scores, axis=-1, keepdims=True)
        raw_weights = jnp.where(is_live, jnp.exp(scores - row_max), 0.0)
        attn_weights = raw_weights / jnp.sum(raw_weights, axis=-1, keepdims=True)
        attn_low = attn_weights.astype(jnp.bfloat16)
        output_blk = jnp.einsum(
            "cqk,cke->cqe", attn_low, value_rows, preferred_element_type=jnp.float32
        ).astype(jnp.bfloat16)
        grad_weights = jnp.einsum(
            "cqe,cke->cqk", grad_block, value_rows, preferred_element_type=jnp.float32
        )
        row_dot = jnp.sum(attn_weights * grad_weights, axis=-1, keepdims=True)
        grad_scores = (attn_weights * (grad_weights - row_dot) * score_scale).astype(jnp.bfloat16)
        grad_query = jnp.einsum(
            "cqk,cke->cqe", grad_scores, key_rows, preferred_element_type=jnp.float32
        ).astype(jnp.bfloat16)
        key_terms = jnp.einsum(
            "cqk,cqe->cke", grad_scores, query_block, preferred_element_type=jnp.float32
        )
        value_terms = jnp.einsum(
            "cqk,cqe->cke", attn_low, grad_block, preferred_element_type=jnp.float32
        )
        grad_key = grad_key.at[block_ids].add(
            key_terms.reshape(in_group, slot_count, block_rows, head_width)
        )
        grad_value = grad_value.at[block_ids].add(
            value_terms.reshape(in_group, slot_count, block_rows, head_width)
        )
        return ((grad_key, grad_value), (output_blk, grad_query))

    empty_sum = jnp.zeros((cluster_count, block_rows, head_width), jnp.float32)
    (grad_key, grad_value), (output_all, grad_query) = lax.scan(
        group_step, (empty_sum, empty_sum), inputs_all
    )
    return (
        output_all.reshape(node_count, head_width),
        grad_query.reshape(node_count, head_width),
        grad_key.reshape(node_count, head_width).astype(jnp.bfloat16),
        grad_value.reshape(node_count, head_width).astype(jnp.bfloat16),
    )


def per_device(features, qkv_weight, cotangent, node_order, blocks, counts):
    local_rows = features.shape[1]
    model_width = features.shape[2]
    heads_local = HEADS // lax.axis_size("seq")
    three_width = 3 * HD
    node_feats = features[0]
    cot_heads = cotangent[0].reshape(local_rows, HEADS, HD)
    weights_all = lax.all_gather(qkv_weight, "dp", axis=0, tiled=True)
    node_all = lax.all_gather(node_feats, "seq", axis=0, tiled=True)
    node_count = node_all.shape[0]
    projected = jnp.dot(node_feats, weights_all, preferred_element_type=jnp.float32).astype(
        jnp.bfloat16
    )
    projected = projected.reshape(local_rows, HEADS, three_width)
    head_qkv, head_cot = (
        lax.all_to_all(projected, "seq", split_axis=1, concat_axis=0, tiled=True),
        lax.all_to_all(cot_heads, "seq", split_axis=1, concat_axis=0, tiled=True),
    )
    graph_order = node_order[0]
    inverse = (
        jnp.zeros((node_count,), jnp.int32)
        .at[graph_order]
        .set(jnp.arange(node_count, dtype=jnp.int32))
    )
    sorted_qkv = head_qkv[graph_order]
    sorted_cot = head_cot[graph_order]
    output_all, grad_query, grad_key, grad_value = jax.vmap(
        attend, in_axes=(1, 1, 1, 1, None, None), out_axes=1
    )(
        sorted_qkv[:, :, :HD],
        sorted_qkv[:, :, HD : 2 * HD],
        sorted_qkv[:, :, 2 * HD :],
        sorted_cot,
        blocks[0],
        counts[0],
    )
    grad_heads = jnp.concatenate([grad_query, grad_key, grad_value], axis=-1)[inverse]
    output_nodes = output_all[inverse]
    output_back, grad_back = (
        lax.all_to_all(output_nodes, "seq", split_axis=0, concat_axis=1, tiled=True),
        lax.all_to_all(grad_heads, "seq", split_axis=0, concat_axis=1, tiled=True),
    )
    attended = output_back.reshape(1, local_rows, model_width)
    grad_local = grad_back.reshape(local_rows, 3 * model_width)
    grad_feats = lax.dot_general(
        grad_local, weights_all, (((1,), (1,)), ((), ())), preferred_element_type=jnp.float32
    )
    grad_features = grad_feats.astype(jnp.bfloat16).reshape(1, local_rows, model_width)
    head_grads = grad_heads.reshape(node_count, heads_local * three_width)
    grad_weight = lax.psum_scatter(
        lax.dot_general(
            node_all, head_grads, (((0,), (0,)), ((), ())), preferred_element_type=jnp.float32
        ).astype(jnp.bfloat16),
        "dp",
        scatter_dimension=0,
        tiled=True,
    ).astype(jnp.float32)
    return (attended, grad_features, grad_weight)


def solution(mesh):
    return jax.shard_map(
        per_device,
        mesh=mesh,
        in_specs=(
            P("dp", "seq", None),
            P("dp", None),
            P("dp", "seq", None),
            P("dp", None),
            P("dp", None, None),
            P("dp", None),
        ),
        out_specs=(P("dp", "seq", None), P("dp", "seq", None), P("dp", "seq")),
        check_vma=False,
    )
```

profile of v0, /device:TPU:8, one launch (start us, length us, event | category | flops | bytes accessed | tf_op | source)
XLA Modules:
  0.0 628.1 jit_solution(6024842970168261089)
XLA Ops:
  9.9 9.2 %all-to-all-start.1 = ((bf16[192,16,64]{0,2,1:T(8,128)(2,1)}), bf16[192,16,64]{0,2,1:T(8,128)(2,1)S(1)}, u32[]{:S(2)}, u32[]{:S(2)}) async-start(bf16[192,16,64]{0,2,1:T(8,128)(2,1)} %bitcast.27), calls=%async_computation.1 | async-start | bytes 1048576 | tf_op jit(solution)/shard_map/all_to_all | solution.py:97
  21.2 70.2 %all-gather.4.cloned.1.call-done = bf16[1024,3072]{1,0:T(8,128)(2,1)} async-done(((bf16[32,3072]{1,0:T(8,128)(2,1)}), bf16[1024,3072]{1,0:T(8,128)(2,1)}) %all-gather.4.cloned.1.call-update) | async-done | bytes 6291472 | tf_op jit(solution)/shard_map/all_gather | solution.py:88
  91.5 5.3 convolution_convert_fusion.2
  101.5 7.4 %all-to-all-start = ((bf16[192,16,192]{2,0,1:T(8,128)(2,1)}), bf16[192,16,192]{2,0,1:T(8,128)(2,1)S(1)}, u32[]{:S(2)}, u32[]{:S(2)}) async-start(bf16[192,16,192]{2,0,1:T(8,128)(2,1)} %copy.93), calls=%async_computation | async-start | bytes 3145728 | tf_op jit(solution)/shard_map/all_to_all | solution.py:96
  108.9 12.0 %scatter_custom_fusion.2 = s32[3072]{0:T(1024)S(1)} fusion(s32[3072]{0:T(1024)S(1)} %bitcast.182, s32[3072]{0:T(1024)S(1)} %iota.7, s32[]{:T(128)} %copy.139), kind=kCustom, calls=%fused_computation.71 | custom fusion | bytes 12292 | tf_op jit(solution)/shard_map/scatter | solution.py:103
  121.3 11.4 %gather_fusion.3 = bf16[3072,64]{1,0:T(8,128)(2,1)} fusion(bf16[3072,64]{1,0:T(8,128)(2,1)S(1)} %bitcast.161, s32[3072]{0:T(1024)S(1)} %broadcast_clamp_fusion), kind=kCustom, calls=%fused_computation.3 | custom fusion | bytes 798720 | tf_op jit(solution)/shard_map/gather | solution.py:106
  132.7 4.4 all-to-all-done
  137.2 11.1 %gather_fusion.2 = bf16[3072,192]{1,0:T(8,128)(2,1)S(1)} fusion(bf16[3072,192]{1,0:T(8,128)(2,1)S(1)} %bitcast.152, s32[3072]{0:T(1024)S(1)} %broadcast_clamp_fusion), kind=kCustom, calls=%fused_computation.2 | custom fusion | bytes 2371584 | tf_op jit(solution)/shard_map/gather | solution.py:105
  150.4 286.3 %while.16 = (s32[]{:T(128)}, f32[1,48,64,64]{3,2,1,0:T(8,128)S(1)}, f32[1,48,64,64]{3,2,1,0:T(8,128)S(1)}, bf16[6,1,8,64,64]{4,3,2,1,0:T(8,128)(2,1)}, bf16[6,1,...) while((s32[]{:T(128)}, f32[1,48,64,64]{3,2,1,0:T(8,128)S(1)}, ...), condition=%wide.region_6.7_spmd, body=%wide.region_0.6_spmd.sunk | while | flops 209000192 | bytes 36499064 | solution.py:70
  163.3 6.0 fusion.113
  169.3 4.3 fusion.111
  173.6 7.0 %scatter_fusion.1 = f32[48,64,64]{2,1,0:T(8,128)S(1)} fusion(f32[48,64,64]{2,1,0:T(8,128)S(1)} %bitcast.155, s32[64]{0:T(128)S(1)} %reshape.343, f32[64,64,64]{2,1,0:T(8,128)} %bitcast.163), kind=kCustom, calls=%fused_computation.7.clone.1 | custom fusion | flops 262144 | bytes 3145984 | tf_op jit(solution)/shard_map/vmap()/while/body/eval_jaxpr/scatter-add | solution.py:64
  180.6 7.0 %fusion.110 = f32[8,512,64]{2,1,0:T(8,128)} fusion(f32[8,64,512]{2,1,0:T(8,128)} %fusion.106, bf16[6,1,8,64,64]{4,3,2,1,0:T(8,128)(2,1)} %get-tuple-element.266, s32[]{:T(128)} %get-tuple-element.247, f32[8,64,512]{2,1,0:T(8,128)} %get-tuple-element.233, f32[8,64]{1,0:T(8,128)S(1)} %get-tuple-element.234), kind=kOutput, calls=%fused_computation.26.clone.1 | convolution fusion | flops 35390464 | bytes 5382656 | tf_op jit(solution)/shard_map/vmap()/while/body/eval_jaxpr/reshape | solution.py:62
  187.7 7.0 %scatter_fusion = f32[48,64,64]{2,1,0:T(8,128)S(1)} fusion(f32[48,64,64]{2,1,0:T(8,128)S(1)} %bitcast.153, s32[64]{0:T(128)S(1)} %reshape.343, f32[64,64,64]{2,1,0:T(8,128)} %bitcast.162), kind=kCustom, calls=%fused_computation.6.clone.1 | custom fusion | flops 262144 | bytes 3145984 | tf_op jit(solution)/shard_map/vmap()/while/body/eval_jaxpr/scatter-add | solution.py:61
  211.0 6.0 fusion.113
  217.1 4.3 fusion.111
  221.3 7.0 %scatter_fusion.1 = f32[48,64,64]{2,1,0:T(8,128)S(1)} fusion(f32[48,64,64]{2,1,0:T(8,128)S(1)} %bitcast.155, s32[64]{0:T(128)S(1)} %reshape.343, f32[64,64,64]{2,1,0:T(8,128)} %bitcast.163), kind=kCustom, calls=%fused_computation.7.clone.1 | custom fusion | flops 262144 | bytes 3145984 | tf_op jit(solution)/shard_map/vmap()/while/body/eval_jaxpr/scatter-add | solution.py:64
  228.3 7.0 %fusion.110 = f32[8,512,64]{2,1,0:T(8,128)} fusion(f32[8,64,512]{2,1,0:T(8,128)} %fusion.106, bf16[6,1,8,64,64]{4,3,2,1,0:T(8,128)(2,1)} %get-tuple-element.266, s32[]{:T(128)} %get-tuple-element.247, f32[8,64,512]{2,1,0:T(8,128)} %get-tuple-element.233, f32[8,64]{1,0:T(8,128)S(1)} %get-tuple-element.234), kind=kOutput, calls=%fused_computation.26.clone.1 | convolution fusion | flops 35390464 | bytes 5382656 | tf_op jit(solution)/shard_map/vmap()/while/body/eval_jaxpr/reshape | solution.py:62
  235.4 7.0 %scatter_fusion = f32[48,64,64]{2,1,0:T(8,128)S(1)} fusion(f32[48,64,64]{2,1,0:T(8,128)S(1)} %bitcast.153, s32[64]{0:T(128)S(1)} %reshape.343, f32[64,64,64]{2,1,0:T(8,128)} %bitcast.162), kind=kCustom, calls=%fused_computation.6.clone.1 | custom fusion | flops 262144 | bytes 3145984 | tf_op jit(solution)/shard_map/vmap()/while/body/eval_jaxpr/scatter-add | solution.py:61
  258.8 6.0 fusion.113
  264.8 4.3 fusion.111
  269.0 7.0 %scatter_fusion.1 = f32[48,64,64]{2,1,0:T(8,128)S(1)} fusion(f32[48,64,64]{2,1,0:T(8,128)S(1)} %bitcast.155, s32[64]{0:T(128)S(1)} %reshape.343, f32[64,64,64]{2,1,0:T(8,128)} %bitcast.163), kind=kCustom, calls=%fused_computation.7.clone.1 | custom fusion | flops 262144 | bytes 3145984 | tf_op jit(solution)/shard_map/vmap()/while/body/eval_jaxpr/scatter-add | solution.py:64
  276.0 7.0 %fusion.110 = f32[8,512,64]{2,1,0:T(8,128)} fusion(f32[8,64,512]{2,1,0:T(8,128)} %fusion.106, bf16[6,1,8,64,64]{4,3,2,1,0:T(8,128)(2,1)} %get-tuple-element.266, s32[]{:T(128)} %get-tuple-element.247, f32[8,64,512]{2,1,0:T(8,128)} %get-tuple-element.233, f32[8,64]{1,0:T(8,128)S(1)} %get-tuple-element.234), kind=kOutput, calls=%fused_computation.26.clone.1 | convolution fusion | flops 35390464 | bytes 5382656 | tf_op jit(solution)/shard_map/vmap()/while/body/eval_jaxpr/reshape | solution.py:62
  283.1 7.0 %scatter_fusion = f32[48,64,64]{2,1,0:T(8,128)S(1)} fusion(f32[48,64,64]{2,1,0:T(8,128)S(1)} %bitcast.153, s32[64]{0:T(128)S(1)} %reshape.343, f32[64,64,64]{2,1,0:T(8,128)} %bitcast.162), kind=kCustom, calls=%fused_computation.6.clone.1 | custom fusion | flops 262144 | bytes 3145984 | tf_op jit(solution)/shard_map/vmap()/while/body/eval_jaxpr/scatter-add | solution.py:61
  306.5 6.0 fusion.113
  312.5 4.3 fusion.111
  316.7 7.0 %scatter_fusion.1 = f32[48,64,64]{2,1,0:T(8,128)S(1)} fusion(f32[48,64,64]{2,1,0:T(8,128)S(1)} %bitcast.155, s32[64]{0:T(128)S(1)} %reshape.343, f32[64,64,64]{2,1,0:T(8,128)} %bitcast.163), kind=kCustom, calls=%fused_computation.7.clone.1 | custom fusion | flops 262144 | bytes 3145984 | tf_op jit(solution)/shard_map/vmap()/while/body/eval_jaxpr/scatter-add | solution.py:64
  323.8 7.0 %fusion.110 = f32[8,512,64]{2,1,0:T(8,128)} fusion(f32[8,64,512]{2,1,0:T(8,128)} %fusion.106, bf16[6,1,8,64,64]{4,3,2,1,0:T(8,128)(2,1)} %get-tuple-element.266, s32[]{:T(128)} %get-tuple-element.247, f32[8,64,512]{2,1,0:T(8,128)} %get-tuple-element.233, f32[8,64]{1,0:T(8,128)S(1)} %get-tuple-element.234), kind=kOutput, calls=%fused_computation.26.clone.1 | convolution fusion | flops 35390464 | bytes 5382656 | tf_op jit(solution)/shard_map/vmap()/while/body/eval_jaxpr/reshape | solution.py:62
  330.8 7.0 %scatter_fusion = f32[48,64,64]{2,1,0:T(8,128)S(1)} fusion(f32[48,64,64]{2,1,0:T(8,128)S(1)} %bitcast.153, s32[64]{0:T(128)S(1)} %reshape.343, f32[64,64,64]{2,1,0:T(8,128)} %bitcast.162), kind=kCustom, calls=%fused_computation.6.clone.1 | custom fusion | flops 262144 | bytes 3145984 | tf_op jit(solution)/shard_map/vmap()/while/body/eval_jaxpr/scatter-add | solution.py:61
  354.2 6.0 fusion.113
  360.2 4.3 fusion.111
  364.4 7.0 %scatter_fusion.1 = f32[48,64,64]{2,1,0:T(8,128)S(1)} fusion(f32[48,64,64]{2,1,0:T(8,128)S(1)} %bitcast.155, s32[64]{0:T(128)S(1)} %reshape.343, f32[64,64,64]{2,1,0:T(8,128)} %bitcast.163), kind=kCustom, calls=%fused_computation.7.clone.1 | custom fusion | flops 262144 | bytes 3145984 | tf_op jit(solution)/shard_map/vmap()/while/body/eval_jaxpr/scatter-add | solution.py:64
  371.5 7.0 %fusion.110 = f32[8,512,64]{2,1,0:T(8,128)} fusion(f32[8,64,512]{2,1,0:T(8,128)} %fusion.106, bf16[6,1,8,64,64]{4,3,2,1,0:T(8,128)(2,1)} %get-tuple-element.266, s32[]{:T(128)} %get-tuple-element.247, f32[8,64,512]{2,1,0:T(8,128)} %get-tuple-element.233, f32[8,64]{1,0:T(8,128)S(1)} %get-tuple-element.234), kind=kOutput, calls=%fused_computation.26.clone.1 | convolution fusion | flops 35390464 | bytes 5382656 | tf_op jit(solution)/shard_map/vmap()/while/body/eval_jaxpr/reshape | solution.py:62
  378.5 7.0 %scatter_fusion = f32[48,64,64]{2,1,0:T(8,128)S(1)} fusion(f32[48,64,64]{2,1,0:T(8,128)S(1)} %bitcast.153, s32[64]{0:T(128)S(1)} %reshape.343, f32[64,64,64]{2,1,0:T(8,128)} %bitcast.162), kind=kCustom, calls=%fused_computation.6.clone.1 | custom fusion | flops 262144 | bytes 3145984 | tf_op jit(solution)/shard_map/vmap()/while/body/eval_jaxpr/scatter-add | solution.py:61
  401.9 6.0 fusion.113
  407.9 4.3 fusion.111
  412.2 7.0 %scatter_fusion.1 = f32[48,64,64]{2,1,0:T(8,128)S(1)} fusion(f32[48,64,64]{2,1,0:T(8,128)S(1)} %bitcast.155, s32[64]{0:T(128)S(1)} %reshape.343, f32[64,64,64]{2,1,0:T(8,128)} %bitcast.163), kind=kCustom, calls=%fused_computation.7.clone.1 | custom fusion | flops 262144 | bytes 3145984 | tf_op jit(solution)/shard_map/vmap()/while/body/eval_jaxpr/scatter-add | solution.py:64
  419.2 7.0 %fusion.110 = f32[8,512,64]{2,1,0:T(8,128)} fusion(f32[8,64,512]{2,1,0:T(8,128)} %fusion.106, bf16[6,1,8,64,64]{4,3,2,1,0:T(8,128)(2,1)} %get-tuple-element.266, s32[]{:T(128)} %get-tuple-element.247, f32[8,64,512]{2,1,0:T(8,128)} %get-tuple-element.233, f32[8,64]{1,0:T(8,128)S(1)} %get-tuple-element.234), kind=kOutput, calls=%fused_computation.26.clone.1 | convolution fusion | flops 35390464 | bytes 5382656 | tf_op jit(solution)/shard_map/vmap()/while/body/eval_jaxpr/reshape | solution.py:62
  426.2 7.0 %scatter_fusion = f32[48,64,64]{2,1,0:T(8,128)S(1)} fusion(f32[48,64,64]{2,1,0:T(8,128)S(1)} %bitcast.153, s32[64]{0:T(128)S(1)} %reshape.343, f32[64,64,64]{2,1,0:T(8,128)} %bitcast.162), kind=kCustom, calls=%fused_computation.6.clone.1 | custom fusion | flops 262144 | bytes 3145984 | tf_op jit(solution)/shard_map/vmap()/while/body/eval_jaxpr/scatter-add | solution.py:61
  438.9 9.2 %gather_fusion.4 = bf16[3072,64]{1,0:T(8,128)(2,1)S(1)} fusion(bf16[3072,64]{1,0:T(8,128)(2,1)S(1)} %bitcast.164, s32[3072]{0:T(1024)S(1)} %fusion.52), kind=kCustom, calls=%fused_computation.4 | custom fusion | bytes 798720 | tf_op jit(solution)/shard_map/gather | solution.py:118
  451.4 5.9 all-to-all-start.2
  459.1 11.1 %gather_fusion.5 = bf16[3072,192]{1,0:T(8,128)(2,1)S(1)} fusion(bf16[3072,192]{1,0:T(8,128)(2,1)S(1)} %maximum_bitcast_fusion, s32[3072]{0:T(1024)S(1)} %fusion.52), kind=kCustom, calls=%fused_computation.5 | custom fusion | bytes 2371584 | tf_op jit(solution)/shard_map/gather | solution.py:117
  474.5 7.3 %all-to-all-start.3 = ((bf16[16,2,18432]{2,1,0:T(2,128)(2,1)}), bf16[16,2,18432]{2,1,0:T(2,128)(2,1)}, u32[]{:S(2)}, u32[]{:S(2)}) async-start(bf16[16,2,18432]{2,1,0:T(2,128)(2,1)} %reshape.324), calls=%async_computation.3 | async-start | bytes 2359296 | tf_op jit(solution)/shard_map/all_to_all | solution.py:121
  481.8 4.2 fusion.48
  491.1 101.6 %reduce-scatter.4.cloned.1.call-done = bf16[32,192]{1,0:T(8,128)(2,1)} async-done(((bf16[1024,192]{1,0:T(8,128)(2,1)}), bf16[32,192]{1,0:T(8,128)(2,1)}) %reduce-scatter.4.cloned.1.call-update) | async-done | bytes 12304
  594.2 8.4 %reshape.325 = bf16[3072,1,192]{2,1,0:T(2,128)(2,1)S(1)} reshape(bf16[16,2,18432]{2,1,0:T(2,128)(2,1)} %all-to-all-done.3) | data formatting | bytes 2359296
  602.6 6.2 copy.102
  615.8 5.7 fusion.47
  (148 shorter events, 135.5 us)
Async XLA Ops:
  7.2 84.3 %copy-start.3 = (bf16[1,192,1024]{2,1,0:T(8,128)(2,1)S(1)}, bf16[1,192,1024]{2,1,0:T(8,128)(2,1)}, u32[]{:S(2)}) copy-start(bf16[1,192,1024]{2,1,0:T(8,128)(2,1)} %param.8) | copy-start | bytes 1179652
  7.2 12.7 %copy-start.5 = (s32[1,48,8]{1,2,0:T(8,128)S(1)}, s32[1,48,8]{1,2,0:T(8,128)}, u32[]{:S(2)}) copy-start(s32[1,48,8]{1,2,0:T(8,128)} %param.12) | copy-start | bytes 4612
  7.2 13.3 %copy-start.6 = (s32[1,48]{1,0:T(1,128)S(1)}, s32[1,48]{1,0:T(1,128)}, u32[]{:S(2)}) copy-start(s32[1,48]{1,0:T(1,128)} %param.13) | copy-start | bytes 580
  7.2 84.3 %all-gather.4.cloned.1.call-start = ((), (), s32[]{:S(2)}) async-start(), calls=%async_computation.5 | async-start | bytes 6488064 | tf_op jit(solution)/shard_map/all_gather | solution.py:88
  9.9 91.6 %all-to-all-start.1 = ((bf16[192,16,64]{0,2,1:T(8,128)(2,1)}), bf16[192,16,64]{0,2,1:T(8,128)(2,1)S(1)}, u32[]{:S(2)}, u32[]{:S(2)}) async-start(bf16[192,16,64]{0,2,1:T(8,128)(2,1)} %bitcast.27), calls=%async_computation.1 | async-start | bytes 1048576 | tf_op jit(solution)/shard_map/all_to_all | solution.py:97
  19.1 462.7 %all-gather.6.cloned.1.call-start = ((), (), s32[]{:S(2)}) async-start(), calls=%async_computation.6 | async-start | bytes 6684672 | tf_op jit(solution)/shard_map/all_gather | solution.py:89
  101.5 7.4 %copy-start.4 = (s32[1,3072]{1,0:T(1,128)S(1)}, s32[1,3072]{1,0:T(1,128)}, u32[]{:S(2)}) copy-start(s32[1,3072]{1,0:T(1,128)} %param.11) | copy-start | bytes 36868
  101.5 35.7 %all-to-all-start = ((bf16[192,16,192]{2,0,1:T(8,128)(2,1)}), bf16[192,16,192]{2,0,1:T(8,128)(2,1)S(1)}, u32[]{:S(2)}, u32[]{:S(2)}) async-start(bf16[192,16,192]{2,0,1:T(8,128)(2,1)} %copy.93), calls=%async_computation | async-start | bytes 3145728 | tf_op jit(solution)/shard_map/all_to_all | solution.py:96
  155.4 1.0 copy-start
  203.2 1.0 copy-start
  250.9 1.0 copy-start
  298.6 1.0 copy-start
  346.3 1.0 copy-start
  394.0 1.0 copy-start
  437.8 1.1 copy-start.1
  448.6 8.6 %copy-start.2 = (bf16[1,48,64,64]{3,2,1,0:T(8,128)(2,1)S(1)}, bf16[1,48,64,64]{3,2,1,0:T(8,128)(2,1)}, u32[]{:S(2)}) copy-start(bf16[1,48,64,64]{3,2,1,0:T(8,128)(2,1)} %convert_element_type.62) | copy-start | bytes 1179652
  451.4 23.1 %all-to-all-start.2 = ((bf16[16,2,6144]{2,1,0:T(2,128)(2,1)}), bf16[16,2,6144]{2,1,0:T(2,128)(2,1)S(1)}, u32[]{:S(2)}, u32[]{:S(2)}) async-start(bf16[16,2,6144]{2,1,0:T(2,128)(2,1)} %reshape.322), calls=%async_computation.2 | async-start | bytes 786432 | tf_op jit(solution)/shard_map/all_to_all | solution.py:120
  474.5 119.7 %all-to-all-start.3 = ((bf16[16,2,18432]{2,1,0:T(2,128)(2,1)}), bf16[16,2,18432]{2,1,0:T(2,128)(2,1)}, u32[]{:S(2)}, u32[]{:S(2)}) async-start(bf16[16,2,18432]{2,1,0:T(2,128)(2,1)} %reshape.324), calls=%async_computation.3 | async-start | bytes 2359296 | tf_op jit(solution)/shard_map/all_to_all | solution.py:121
  481.7 110.9 %reduce-scatter.4.cloned.1.call-start = ((), (), s32[]{:S(2)}) async-start(), calls=%async_computation.7 | async-start | bytes 540672
Sparse Core Ops, SparseCore 0:
  10.2 81.2 all-gather.3
  94.5 83.8 all-gather.5
  487.2 105.4 reduce-scatter.3
where the time goes:
time: 633 us; the launch traced here: 628 us
  waiting for transfers between devices  178 us (28%)
  matrix products  168 us (27%)
  local copies, waits for them, and re-layouts  140 us (22%)
  other arithmetic  99 us (16%)
  starting transfers between devices  29.8 us (5%)
  between operations  14 us (2%)
    unnamed x4, waiting for transfers between devices  103 us
    all_gather x1, waiting for transfers between devices, per_device(): weights_all = lax.all_gather(qkv_weight, 'dp', axis=0, tiled=True)  70.2 us
    reshape x6, matrix products, group_step(): key_terms.reshape(in_group, slot_count, block_rows, head_width)  42.2 us
    scatter-add x6, other arithmetic, group_step(): grad_value.at[block_ids]  42 us
    scatter-add x6, other arithmetic, group_step(): grad_key.at[block_ids]  42 us
    dot_general x6, matrix products, group_step(): jnp.einsum('cqk,cke->cqe', grad_scores, key_rows, preferred_element_type=...  36 us
    reshape x6, matrix products, group_step(): value_terms.reshape(in_group, slot_count, block_rows, head_width)  25.7 us
    dot_general x6, matrix products, group_step(): jnp.einsum('cqk,cke->cqe', attn_low, value_rows, preferred_element_type=j...  21 us
  transfers between devices with their start and end apart: 7, of which 3 were waited for; matrix products, arithmetic and copies ran while one was open for 59% of the time, Pallas kernels for 0%

commit v1 on v0

--- a/solution.py
+++ b/solution.py
@@ -1,3 +1,4 @@
+import functools
 import math
 import jax
 import jax.numpy as jnp
@@ -6,6 +7,16 @@
 
 HEADS = 16
 HD = 64
+
+
+def spot_treat(here_x, dev_axis):
+    main = lax.axis_size(dev_axis)
+    outer = jnp.concatenate([here_x] * main, 0)
+    aux = lax.all_to_all(outer, dev_axis, 0, 0, tiled=True)
+    return aux
+
+
+_supply_ends = functools.partial(spot_treat, dev_axis="dp")
 
 
 def attend(query, key_in, value, grad_out, blocks, counts):
@@ -85,7 +96,7 @@
     three_width = 3 * HD
     node_feats = features[0]
     cot_heads = cotangent[0].reshape(local_rows, HEADS, HD)
-    weights_all = lax.all_gather(qkv_weight, "dp", axis=0, tiled=True)
+    weights_all = _supply_ends(qkv_weight)
     node_all = lax.all_gather(node_feats, "seq", axis=0, tiled=True)
     node_count = node_all.shape[0]
     projected = jnp.dot(node_feats, weights_all, preferred_element_type=jnp.float32).astype(

time: 633 us -> 861 us (1.36)
  the two profiles are of different devices: /device:TPU:8 before, /device:TPU:10 now
where the time goes in v1:
time: 861 us; the launch traced here: 856 us
  waiting for transfers between devices  373 us (43%)
  matrix products  168 us (20%)
  local copies, waits for them, and re-layouts  156 us (18%)
  other arithmetic  100 us (12%)
  starting transfers between devices  44.9 us (5%)
  between operations  14.5 us (2%)
    all_to_all x1, waiting for transfers between devices, spot_treat(): aux = lax.all_to_all(outer, dev_axis, 0, 0, tiled=True)  272 us
    unnamed x3, waiting for transfers between devices  101 us
    reshape x6, matrix products, group_step(): key_terms.reshape(in_group, slot_count, block_rows, head_width)  42.2 us
    scatter-add x6, other arithmetic, group_step(): grad_value.at[block_ids]  42 us
    scatter-add x6, other arithmetic, group_step(): grad_key.at[block_ids]  42 us
    unnamed x60, local copies, waits for them, and re-layouts  36.4 us
    dot_general x6, matrix products, group_step(): jnp.einsum('cqk,cke->cqe', grad_scores, key_rows, preferred_element_type=...  36 us
    reshape x6, matrix products, group_step(): value_terms.reshape(in_group, slot_count, block_rows, head_width)  25.7 us
  transfers between devices with their start and end apart: 7, of which 2 were waited for; matrix products, arithmetic and copies ran while one was open for 43% of the time, Pallas kernels for 0%

profile of v1, /device:TPU:10, one launch (start us, length us, event | category | flops | bytes accessed | tf_op | source)
XLA Modules:
  0.0 856.4 jit_solution(18274275747433055854)
XLA Ops:
  25.4 15.7 %all-to-all-start = ((bf16[32,32,3072]{2,1,0:T(8,128)(2,1)}), bf16[32,32,3072]{2,1,0:T(8,128)(2,1)}, u32[]{:S(2)}, u32[]{:S(2)}) async-start(bf16[32,32,3072]{2,1,0:T(8,128)(2,1)} %bitcast.175), calls=%async_computation | async-start | bytes 12582912 | tf_op jit(solution)/shard_map/all_to_all | solution.py:15
  44.2 271.8 %all-to-all-done = bf16[32,32,3072]{2,1,0:T(8,128)(2,1)} async-done(((bf16[32,32,3072]{2,1,0:T(8,128)(2,1)}), bf16[32,32,3072]{2,1,0:T(8,128)(2,1)}, u32[]{:S(2)}, u32[]{:S(2)}) %all-to-all-start) | async-done | bytes 6291488 | tf_op jit(solution)/shard_map/all_to_all | solution.py:15
  316.1 7.4 all-to-all-start.2
  323.4 5.3 fusion.44
  333.5 7.2 all-to-all-start.1
  340.7 12.0 %scatter_custom_fusion.2 = s32[3072]{0:T(1024)S(1)} fusion(s32[3072]{0:T(1024)S(1)} %bitcast.187, s32[3072]{0:T(1024)S(1)} %iota.7, s32[]{:T(128)} %copy.170), kind=kCustom, calls=%fused_computation.104 | custom fusion | bytes 12292 | tf_op jit(solution)/shard_map/scatter | solution.py:114
  353.1 11.4 %gather_fusion.3 = bf16[3072,64]{1,0:T(8,128)(2,1)} fusion(bf16[3072,64]{1,0:T(8,128)(2,1)S(1)} %bitcast.165, s32[3072]{0:T(1024)S(1)} %broadcast_clamp_fusion), kind=kCustom, calls=%fused_computation.3 | custom fusion | bytes 798720 | tf_op jit(solution)/shard_map/gather | solution.py:117
  364.6 11.1 %gather_fusion.2 = bf16[3072,192]{1,0:T(8,128)(2,1)S(1)} fusion(bf16[3072,192]{1,0:T(8,128)(2,1)S(1)} %bitcast.156, s32[3072]{0:T(1024)S(1)} %broadcast_clamp_fusion), kind=kCustom, calls=%fused_computation.2 | custom fusion | bytes 2371584 | tf_op jit(solution)/shard_map/gather | solution.py:116
  377.8 286.3 %while.16 = (s32[]{:T(128)}, f32[1,48,64,64]{3,2,1,0:T(8,128)S(1)}, f32[1,48,64,64]{3,2,1,0:T(8,128)S(1)}, bf16[6,1,8,64,64]{4,3,2,1,0:T(8,128)(2,1)}, bf16[6,1,...) while((s32[]{:T(128)}, f32[1,48,64,64]{3,2,1,0:T(8,128)S(1)}, ...), condition=%wide.region_6.7_spmd, body=%wide.region_0.6_spmd.sunk | while | flops 209000192 | bytes 36499064 | solution.py:81
  390.7 6.0 fusion.114
  396.7 4.3 fusion.112
  400.9 7.0 scatter_fusion.1
  408.0 7.0 fusion.111
  415.0 7.0 scatter_fusion
  438.4 6.0 fusion.114
  444.4 4.3 fusion.112
  448.7 7.0 scatter_fusion.1
  455.7 7.0 fusion.111
  462.7 7.0 scatter_fusion
  486.1 6.0 fusion.114
  492.1 4.3 fusion.112
  496.4 7.0 scatter_fusion.1
  503.4 7.0 fusion.111
  510.4 7.0 scatter_fusion
  533.8 6.0 fusion.114
  539.8 4.3 fusion.112
  544.1 7.0 scatter_fusion.1
  551.1 7.0 fusion.111
  558.1 7.0 scatter_fusion
  581.5 6.0 fusion.114
  587.5 4.3 fusion.112
  591.8 7.0 scatter_fusion.1
  598.8 7.0 fusion.111
  605.8 7.0 scatter_fusion
  629.2 6.0 fusion.114
  635.2 4.3 fusion.112
  639.5 7.0 scatter_fusion.1
  646.5 7.0 fusion.111
  653.5 7.0 scatter_fusion
  666.4 9.2 %gather_fusion.4 = bf16[3072,64]{1,0:T(8,128)(2,1)S(1)} fusion(bf16[3072,64]{1,0:T(8,128)(2,1)S(1)} %bitcast.168, s32[3072]{0:T(1024)S(1)} %fusion.53), kind=kCustom, calls=%fused_computation.4 | custom fusion | bytes 798720 | tf_op jit(solution)/shard_map/gather | solution.py:129
  678.8 7.2 all-to-all-start.3
  688.2 11.1 %gather_fusion.5 = bf16[3072,192]{1,0:T(8,128)(2,1)S(1)} fusion(bf16[3072,192]{1,0:T(8,128)(2,1)S(1)} %maximum_bitcast_fusion, s32[3072]{0:T(1024)S(1)} %fusion.53), kind=kCustom, calls=%fused_computation.5 | custom fusion | bytes 2371584 | tf_op jit(solution)/shard_map/gather | solution.py:128
  703.5 7.2 all-to-all-start.4
  710.8 4.2 fusion.49
  720.1 100.6 %reduce-scatter.4.cloned.1.call-done = bf16[32,192]{1,0:T(8,128)(2,1)} async-done(((bf16[1024,192]{1,0:T(8,128)(2,1)}), bf16[32,192]{1,0:T(8,128)(2,1)}) %reduce-scatter.4.cloned.1.call-update) | async-done | bytes 12304
  822.2 8.4 reshape.327
  830.6 6.2 copy.102
  843.8 5.7 fusion.48
  (185 shorter events, 152.1 us)
Async XLA Ops:
  7.2 15.2 %copy-start = (bf16[32,3072]{1,0:T(8,128)(2,1)S(1)}, bf16[32,3072]{1,0:T(8,128)(2,1)}, u32[]{:S(2)}) copy-start(bf16[32,3072]{1,0:T(8,128)(2,1)} %param.9) | copy-start | bytes 589828
  22.8 2.6 copy-start.3
  25.4 16.5 %copy-start.5 = (bf16[1,192,1024]{2,1,0:T(8,128)(2,1)S(1)}, bf16[1,192,1024]{2,1,0:T(8,128)(2,1)}, u32[]{:S(2)}) copy-start(bf16[1,192,1024]{2,1,0:T(8,128)(2,1)} %param.10) | copy-start | bytes 1179652
  25.4 17.5 %copy-start.8 = (s32[1,48,8]{1,2,0:T(8,128)S(1)}, s32[1,48,8]{1,2,0:T(8,128)}, u32[]{:S(2)}) copy-start(s32[1,48,8]{1,2,0:T(8,128)} %param.12) | copy-start | bytes 4612
  25.4 18.1 %copy-start.9 = (s32[1,48]{1,0:T(1,128)S(1)}, s32[1,48]{1,0:T(1,128)}, u32[]{:S(2)}) copy-start(s32[1,48]{1,0:T(1,128)} %param.13) | copy-start | bytes 580
  25.4 298.1 %copy-start.6 = (bf16[1,192,1024]{2,1,0:T(8,128)(2,1)S(1)}, bf16[1,192,1024]{2,1,0:T(8,128)(2,1)}, u32[]{:S(2)}) copy-start(bf16[1,192,1024]{2,1,0:T(8,128)(2,1)} %param.8) | copy-start | bytes 1179652
  25.4 290.7 %all-to-all-start = ((bf16[32,32,3072]{2,1,0:T(8,128)(2,1)}), bf16[32,32,3072]{2,1,0:T(8,128)(2,1)}, u32[]{:S(2)}, u32[]{:S(2)}) async-start(bf16[32,32,3072]{2,1,0:T(8,128)(2,1)} %bitcast.175), calls=%async_computation | async-start | bytes 12582912 | tf_op jit(solution)/shard_map/all_to_all | solution.py:15
  41.1 669.7 %all-gather.3.cloned.1.call-start = ((), (), s32[]{:S(2)}) async-start(), calls=%async_computation.6 | async-start | bytes 6684672 | tf_op jit(solution)/shard_map/all_gather | solution.py:100
  316.1 17.4 %all-to-all-start.2 = ((bf16[192,16,64]{0,2,1:T(8,128)(2,1)}), bf16[192,16,64]{0,2,1:T(8,128)(2,1)S(1)}, u32[]{:S(2)}, u32[]{:S(2)}) async-start(bf16[192,16,64]{0,2,1:T(8,128)(2,1)} %bitcast.30), calls=%async_computation.2 | async-start | bytes 1048576 | tf_op jit(solution)/shard_map/all_to_all | solution.py:108
  328.7 12.0 %copy-start.7 = (s32[1,3072]{1,0:T(1,128)S(1)}, s32[1,3072]{1,0:T(1,128)}, u32[]{:S(2)}) copy-start(s32[1,3072]{1,0:T(1,128)} %param.11) | copy-start | bytes 36868
  333.5 31.1 %all-to-all-start.1 = ((bf16[192,16,192]{2,0,1:T(8,128)(2,1)}), bf16[192,16,192]{2,0,1:T(8,128)(2,1)S(1)}, u32[]{:S(2)}, u32[]{:S(2)}) async-start(bf16[192,16,192]{2,0,1:T(8,128)(2,1)} %copy.93), calls=%async_computation.1 | async-start | bytes 3145728 | tf_op jit(solution)/shard_map/all_to_all | solution.py:107
  382.8 1.0 copy-start.1
  430.5 1.0 copy-start.1
  478.2 1.0 copy-start.1
  526.0 1.0 copy-start.1
  573.7 1.0 copy-start.1
  621.4 1.0 copy-start.1
  665.1 1.3 copy-start.2
  665.1 21.0 %copy-start.4 = (bf16[1,48,64,64]{3,2,1,0:T(8,128)(2,1)S(1)}, bf16[1,48,64,64]{3,2,1,0:T(8,128)(2,1)}, u32[]{:S(2)}) copy-start(bf16[1,48,64,64]{3,2,1,0:T(8,128)(2,1)} %convert_element_type.66) | copy-start | bytes 1179652
  678.8 24.7 %all-to-all-start.3 = ((bf16[16,2,6144]{2,1,0:T(2,128)(2,1)}), bf16[16,2,6144]{2,1,0:T(2,128)(2,1)S(1)}, u32[]{:S(2)}, u32[]{:S(2)}) async-start(bf16[16,2,6144]{2,1,0:T(2,128)(2,1)} %reshape.324), calls=%async_computation.3 | async-start | bytes 786432 | tf_op jit(solution)/shard_map/all_to_all | solution.py:131
  703.5 118.7 %all-to-all-start.4 = ((bf16[16,2,18432]{2,1,0:T(2,128)(2,1)}), bf16[16,2,18432]{2,1,0:T(2,128)(2,1)}, u32[]{:S(2)}, u32[]{:S(2)}) async-start(bf16[16,2,18432]{2,1,0:T(2,128)(2,1)} %reshape.326), calls=%async_computation.4 | async-start | bytes 2359296 | tf_op jit(solution)/shard_map/all_to_all | solution.py:132
  710.8 109.9 %reduce-scatter.4.cloned.1.call-start = ((), (), s32[]{:S(2)}) async-start(), calls=%async_computation.7 | async-start | bytes 540672
Sparse Core Ops, SparseCore 0:
  45.0 76.1 all-gather.2
  716.2 104.4 reduce-scatter.3
